TPU v7x, 32 devices: a whole 2x2x4 slice. The times are simulated.
32 devices in a mesh: tensor: 8 (over z, core), example: 4 (over y, x).
Axes of the slice: x: 2, y: 2, z: 4, core: 2. Of those that a mesh axis runs over, the one named last changes fastest.
Arguments:
- acts: bfloat16 [256, 8192], P(None, 'example'), may hold values from -6 to 6
- out_grad: bfloat16 [256, 8192], P(None, 'example'), may hold values from -6 to 6
- w_gate: bfloat16 [8192, 28672], P('example', 'tensor'), may hold values from -0.0625 to 0.0625
- w_up: bfloat16 [8192, 28672], P('example', 'tensor'), may hold values from -0.0625 to 0.0625
- w_down: bfloat16 [28672, 8192], P('tensor', 'example'), may hold values from -0.03125 to 0.03125
- proj_in: bfloat16 [8192, 64], P('example'), may hold values from -0.0625 to 0.0625
- proj_gate: bfloat16 [28672, 64], P('tensor'), may hold values from -0.03125 to 0.03125
- proj_up: bfloat16 [28672, 64], P('tensor'), may hold values from -0.03125 to 0.03125
- proj_hidden: bfloat16 [28672, 64], P('tensor'), may hold values from -0.03125 to 0.03125
- proj_out: bfloat16 [8192, 64], P('example'), may hold values from -0.0625 to 0.0625
- store: bfloat16 [4096, 12288], P(('tensor', 'example')), may hold values from -0.0546875 to 0.0546875
- doc_ids: int32 [32, 128], P(('tensor', 'example')), may hold values from 0 to 127, each once within a row
Outputs:
- scores: float32 [4, 4096], P(None, ('tensor', 'example'))
Inputs may be any that keep to these rules, and one draw needn't show every extreme that they name: Each row of doc_ids is a permutation of 0 to 127.
All inputs are finite; a program needn't handle non-finite values.
Results may differ from a plain program's by a relative error of at most 0.022.
Values may be sent and summed in bfloat16 or wider, within the bound.
No kernel may reach another device: no remote copies, remote signals or barrier semaphores. Data moves between devices by JAX's collectives and lax.ppermute only.
A program may use at most 128 MiB of HBM per device.

v0:
```python
import jax
import jax.numpy as jnp
from jax import lax
from jax.sharding import PartitionSpec as P

SEQ_LEN = 64


def grads_of(gate, up, grad_hidden):
    sig = jax.nn.sigmoid(gate)
    hidden = gate * sig * up
    grad_up = grad_hidden * gate * sig
    grad_gate = grad_hidden * up * sig * (1.0 + gate * (1.0 - sig))
    return (
        hidden.astype(jnp.bfloat16),
        grad_gate.astype(jnp.bfloat16),
        grad_up.astype(jnp.bfloat16),
    )


def outer_sums(left, right):
    count = left.shape[0] // SEQ_LEN
    left_seq = left.reshape(count, SEQ_LEN, left.shape[1])
    right_seq = right.reshape(count, SEQ_LEN, right.shape[1])
    total = jnp.einsum("stq,str->sqr", left_seq, right_seq, precision=lax.Precision.HIGHEST)
    return total.reshape(count, left.shape[1] * right.shape[1])


def query_of(in_proj, gate_proj, up_proj, hidden_proj, out_proj):
    return jnp.concatenate(
        [
            outer_sums(in_proj, gate_proj),
            outer_sums(in_proj, up_proj),
            outer_sums(hidden_proj, out_proj),
        ],
        axis=1,
    )


def local(
    acts,
    out_grad,
    w_gate,
    w_up,
    w_down,
    proj_in,
    proj_gate,
    proj_up,
    proj_hidden,
    proj_out,
    store,
    doc_ids,
):
    width = w_gate.shape[1]
    rank = proj_in.shape[1]
    contract_last = (((1,), (1,)), ((), ()))
    left_weights = jnp.concatenate([w_gate, w_up, proj_in], axis=1)
    forward = jnp.dot(acts, left_weights, preferred_element_type=jnp.float32)
    backward = lax.dot_general(out_grad, w_down, contract_last, preferred_element_type=jnp.float32)
    outward = jnp.dot(out_grad, proj_out, preferred_element_type=jnp.float32)
    summed = lax.psum_scatter(
        jnp.concatenate([forward, backward, outward], axis=1).astype(jnp.bfloat16),
        "example",
        scatter_dimension=0,
        tiled=True,
    ).astype(jnp.float32)
    gate = summed[:, :width]
    up = summed[:, width : 2 * width]
    in_proj = summed[:, 2 * width : 2 * width + rank]
    grad_hidden = summed[:, 2 * width + rank : 3 * width + rank]
    out_proj = summed[:, 3 * width + rank :]
    hidden, grad_gate, grad_up = grads_of(gate, up, grad_hidden)
    gate_part = jnp.dot(grad_gate, proj_gate, preferred_element_type=jnp.float32)
    up_part = jnp.dot(grad_up, proj_up, preferred_element_type=jnp.float32)
    hidden_part = jnp.dot(hidden, proj_hidden, preferred_element_type=jnp.float32)
    gate_proj, up_proj, hidden_proj = (
        lax.psum(gate_part.astype(jnp.bfloat16), "tensor").astype(jnp.float32),
        lax.psum(up_part.astype(jnp.bfloat16), "tensor").astype(jnp.float32),
        lax.psum(hidden_part.astype(jnp.bfloat16), "tensor").astype(jnp.float32),
    )
    own_query = query_of(in_proj, gate_proj, up_proj, hidden_proj, out_proj).astype(jnp.bfloat16)
    query = lax.all_gather(own_query, "example", axis=0, tiled=True)
    picked = jnp.take(store, doc_ids[0], axis=0)
    return lax.dot_general(query, picked, contract_last, preferred_element_type=jnp.float32)


def solution(mesh):
    return jax.shard_map(
        local,
        mesh=mesh,
        in_specs=(
            P(None, "example"),
            P(None, "example"),
            P("example", "tensor"),
            P("example", "tensor"),
            P("tensor", "example"),
            P("example", None),
            P("tensor", None),
            P("tensor", None),
            P("tensor", None),
            P("example", None),
            P(("tensor", "example"), None),
            P(("tensor", "example"), None),
        ),
        out_specs=P(None, ("tensor", "example")),
        check_vma=False,
    )
```

profile of v0, /device:TPU:0, one launch (start us, length us, event | category | flops | bytes accessed | tf_op | source)
XLA Modules:
  0.0 193.3 jit_solution(8513815710191261834)
XLA Ops:
  6.5 0.0 copy-start
  6.5 0.0 reduce-scatter.4.cloned.1.call-start
  6.5 2.1 %copy.17 = bf16[2048,64]{1,0:T(8,128)(2,1)} copy(bf16[2048,64]{0,1:T(8,128)(2,1)} %param.17) | data formatting | bytes 524288 | tf_op args[5]
  8.6 0.0 copy-start.1
  8.6 0.0 copy-start.3
  8.6 0.0 copy-start.2
  8.6 0.0 copy-start.4
  8.7 9.7 %convolution_convert_fusion = bf16[256,3584]{0,1:T(8,128)(2,1)S(1)} fusion(bf16[256,2048]{1,0:T(8,128)(2,1)} %param.13, bf16[3584,2048]{1,0:T(8,128)(2,1)} %param.16), kind=kOutput, calls=%fused_computation.10 | convolution fusion | flops 3759013888 | bytes 17563648 | tf_op jit(solution)/shard_map/dot_general | solution.py:59
  18.3 0.0 copy-done.1
  18.3 0.0 copy-done.3
  18.3 0.4 convolution_convert_fusion.1
  18.8 0.0 copy-done.2
  18.8 0.0 copy-done.4
  18.8 14.2 %fusion.9 = bf16[256,7232]{0,1:T(8,128)(2,1)S(1)} fusion(bf16[256,2048]{1,0:T(8,128)(2,1)S(1)} %copy-done.4, bf16[2048,64]{1,0:T(8,128)(2,1)S(1)} %copy-done.2, bf16[2048,3584]{1,0:T(8,128)(2,1)} %param.15, bf16[2048,3584]{1,0:T(8,128)(2,1)} %param.14), kind=kOutput, calls=%fused_computation.8 | convolution fusion | flops 7674019840 | bytes 34373632 | tf_op jit(solution)/shard_map/dot_general | solution.py:58
  33.0 25.2 %pad_maximum_fusion = bf16[256,10880]{0,1:T(8,128)(2,1)} fusion(bf16[256,64]{0,1:T(8,128)(2,1)S(1)} %convolution_convert_fusion.1, bf16[256,3584]{0,1:T(8,128)(2,1)S(1)} %convolution_convert_fusion, bf16[256,7232]{0,1:T(8,128)(2,1)S(1)} %fusion.9), kind=kLoop, calls=%fused_computation.9 | loop fusion | flops 16711680 | bytes 11141120 | tf_op jit(solution)/shard_map/concatenate | solution.py:62
  58.2 8.3 %copy.20 = bf16[256,10880]{1,0:T(8,128)(2,1)} copy(bf16[256,10880]{0,1:T(8,128)(2,1)} %pad_maximum_fusion) | data formatting | bytes 11141120
  66.5 0.0 copy-start.8
  66.5 0.0 reduce-scatter.4.cloned.1.call-update
  66.5 0.6 copy-done.8
  67.2 0.0 copy-done
  67.2 4.2 %gather_fusion = bf16[128,12288]{1,0:T(8,128)(2,1)} fusion(bf16[128,12288]{1,0:T(8,128)(2,1)S(1)} %copy-done, s32[1024]{0:T(1024)S(1)} %pad_clamp_fusion), kind=kCustom, calls=%fused_computation | custom fusion | bytes 6291968 | tf_op jit(solution)/shard_map/jit(_take)/gather | solution.py:83
  71.4 62.1 %reduce-scatter.4.cloned.1.call-done = bf16[64,10880]{1,0:T(8,128)(2,1)} async-done(((bf16[256,10880]{1,0:T(8,128)(2,1)}), bf16[64,10880]{1,0:T(8,128)(2,1)}) %reduce-scatter.4.cloned.1.call-update) | async-done | bytes 1392656
  133.5 4.0 %copy.21 = bf16[64,10880]{0,1:T(8,128)(2,1)} copy(bf16[64,10880]{1,0:T(8,128)(2,1)} %reduce-scatter.4.cloned.1.call-done) | data formatting | bytes 2785280
  137.5 0.0 copy-start.5
  137.5 2.0 %convert_element_type.34 = f32[64,10880]{0,1:T(8,128)S(1)} convert(bf16[64,10880]{0,1:T(8,128)(2,1)} %copy.21) | non-fusion elementwise | flops 696320 | bytes 4177920 | tf_op jit(solution)/shard_map/convert_element_type | solution.py:66
  139.5 0.0 copy-done.5
  139.6 0.0 copy-start.6
  139.6 0.7 convolution_convert_fusion.2
  140.3 0.3 copy-done.6
  140.6 0.0 copy-start.7
  140.6 0.7 convolution_convert_fusion.3
  141.3 0.3 copy-done.7
  141.6 0.9 convolution_convert_fusion.4
  142.5 29.0 %all-reduce = (bf16[64,64]{1,0:T(8,128)(2,1)S(1)}, bf16[64,64]{1,0:T(8,128)(2,1)S(1)}, bf16[64,64]{1,0:T(8,128)(2,1)S(1)}) all-reduce(bf16[64,64]{1,0:T(8,128)(2,1)S(1)} %convolution_convert_fusion.2, bf16[64,64]{1,0:T(8,128)(2,1)S(1)} %convolution_convert_fusion.3, ...), channel_id=1, replica_groups=mesh['tensor'=8,'example'=4] {'tensor'}, use_global_device_ids=true, to_apply=%region_3.0 | all-reduce | flops 12288 | bytes 49152 | tf_op jit(solution)/shard_map/psum | solution.py:79
  171.5 0.8 convolution_convert_fusion.7
  172.4 0.1 concatenate.27
  172.5 0.8 convolution_convert_fusion.6
  173.3 0.1 concatenate.28
  173.4 0.9 convolution_convert_fusion.5
  174.3 0.1 concatenate.29
  174.4 0.1 maximum_bitcast_fusion
  174.5 8.5 %all-gather = bf16[4,1,12288]{2,1,0:T(2,128)(2,1)S(1)} all-gather(bf16[1,1,12288]{2,1,0:T(2,128)(2,1)S(1)} %maximum_bitcast_fusion), channel_id=1, replica_groups=mesh['tensor'=8,'example'=4] {'example'}, dimensions={0}, use_global_device_ids=true | all-gather | bytes 122880 | tf_op jit(solution)/shard_map/all_gather | solution.py:82
  183.0 3.5 %fusion.12 = f32[4,128]{1,0:T(4,128)} fusion(bf16[128,12288]{1,0:T(8,128)(2,1)} %gather_fusion, pred[128]{0:T(512)(128)(4,1)S(1)} %compare_and_fusion, bf16[4,1,12288]{2,1,0:T(2,128)(2,1)S(1)} %all-gather), kind=kOutput, calls=%fused_computation.11 | convolution fusion | flops 14155776 | bytes 3246208 | tf_op jit(solution)/shard_map/dot_general | solution.py:84
  (3 shorter events, 0.0 us)
Async XLA Ops:
  6.5 60.6 %copy-start = (bf16[128,12288]{1,0:T(8,128)(2,1)S(1)}, bf16[128,12288]{1,0:T(8,128)(2,1)}, u32[]{:S(2)}) copy-start(bf16[128,12288]{1,0:T(8,128)(2,1)} %param.22) | copy-start | bytes 9437188
  6.5 127.0 %reduce-scatter.4.cloned.1.call-start = ((), (), s32[]{:S(2)}) async-start(), calls=%async_computation.1 | async-start | bytes 6963200
  8.6 9.7 %copy-start.1 = (bf16[256,2048]{1,0:T(8,128)(2,1)S(1)}, bf16[256,2048]{1,0:T(8,128)(2,1)}, u32[]{:S(2)}) copy-start(bf16[256,2048]{1,0:T(8,128)(2,1)} %param.13) | copy-start | bytes 3145732
  8.6 9.7 %copy-start.3 = (bf16[2048,64]{0,1:T(8,128)(2,1)S(1)}, bf16[2048,64]{0,1:T(8,128)(2,1)}, u32[]{:S(2)}) copy-start(bf16[2048,64]{0,1:T(8,128)(2,1)} %param.21) | copy-start | bytes 786436
  8.6 10.1 %copy-start.2 = (bf16[2048,64]{1,0:T(8,128)(2,1)S(1)}, bf16[2048,64]{1,0:T(8,128)(2,1)}, u32[]{:S(2)}) copy-start(bf16[2048,64]{1,0:T(8,128)(2,1)} %copy.17) | copy-start | bytes 786436
  8.6 10.2 %copy-start.4 = (bf16[256,2048]{1,0:T(8,128)(2,1)S(1)}, bf16[256,2048]{1,0:T(8,128)(2,1)}, u32[]{:S(2)}) copy-start(bf16[256,2048]{1,0:T(8,128)(2,1)} %param.12) | copy-start | bytes 3145732
  66.5 0.7 copy-start.8
  137.5 2.0 %copy-start.5 = (bf16[3584,64]{0,1:T(8,128)(2,1)S(1)}, bf16[3584,64]{0,1:T(8,128)(2,1)}, u32[]{:S(2)}) copy-start(bf16[3584,64]{0,1:T(8,128)(2,1)} %param.20) | copy-start | bytes 1376260
  139.6 1.0 copy-start.6
  140.6 1.0 copy-start.7
Sparse Core Ops, SparseCore 0:
  66.6 66.8 reduce-scatter.3
where the time goes:
time: 194 us; the launch traced here: 193 us
  waiting for transfers between devices  62.2 us (32%)
  blocking collectives  37.6 us (19%)
  matrix products  32.7 us (17%)
  other arithmetic  27.3 us (14%)
  local copies, waits for them, and re-layouts  20.1 us (10%)
  between operations  13.5 us (7%)
    unnamed x2, waiting for transfers between devices  62.2 us
    psum x1, blocking collectives, local(): lax.psum(hidden_part.astype(jnp.bfloat16), 'tensor').astype(jnp.float32)  29 us
    concatenate x1, other arithmetic, local(): jnp.concatenate([forward, backward, outward], axis=1).astype(jnp.bfloat16)  25.2 us
    unnamed x21, local copies, waits for them, and re-layouts  15.6 us
    dot_general x1, matrix products, local(): forward = jnp.dot(acts, left_weights, preferred_element_type=jnp.float32)  14.2 us
    dot_general x1, matrix products, local(): lax.dot_general(out_grad, w_down, contract_last, preferred_element_type=j...  9.66 us
    all_gather x1, blocking collectives, local(): query = lax.all_gather(own_query, 'example', axis=0, tiled=True)  8.53 us
    gather x1, local copies, waits for them, and re-layouts, local(): picked = jnp.take(store, doc_ids[0], axis=0)  4.22 us
  transfers between devices with their start and end apart: 1, of which 1 were waited for; matrix products, arithmetic and copies ran while one was open for 2% of the time, Pallas kernels for 0%

commit v1 on v0

--- a/solution.py
+++ b/solution.py
@@ -4,6 +4,11 @@
 from jax.sharding import PartitionSpec as P
 
 SEQ_LEN = 64
+
+
+def add_all(x, axis):
+    parts = lax.all_gather(x, axis)
+    return jnp.sum(parts, axis=0)
 
 
 def grads_of(gate, up, grad_hidden):
@@ -76,7 +81,7 @@
     gate_proj, up_proj, hidden_proj = (
         lax.psum(gate_part.astype(jnp.bfloat16), "tensor").astype(jnp.float32),
         lax.psum(up_part.astype(jnp.bfloat16), "tensor").astype(jnp.float32),
-        lax.psum(hidden_part.astype(jnp.bfloat16), "tensor").astype(jnp.float32),
+        add_all(hidden_part.astype(jnp.bfloat16), "tensor").astype(jnp.float32),
     )
     own_query = query_of(in_proj, gate_proj, up_proj, hidden_proj, out_proj).astype(jnp.bfloat16)
     query = lax.all_gather(own_query, "example", axis=0, tiled=True)

time: 194 us -> 211 us (1.088)
  blocking collectives: 37.6 us -> 51.1 us
    all_gather x0 -> x1, blocking collectives: none -> 14 us  [add_all(): parts = lax.all_gather(x, axis)]
    dot_general x1, matrix products: 0.72 us -> 2.85 us  [local(): jnp.dot(hidden, proj_hidden, preferred_element_type=jnp.float32)]
where the time goes in v1:
time: 211 us; the launch traced here: 210 us
  waiting for transfers between devices  62.2 us (29%)
  blocking collectives  51.1 us (24%)
  matrix products  34.8 us (16%)
  other arithmetic  27.4 us (13%)
  local copies, waits for them, and re-layouts  21.3 us (10%)
  between operations  13.5 us (6%)
    unnamed x2, waiting for transfers between devices  62.2 us
    psum x1, blocking collectives, local(): lax.psum(up_part.astype(jnp.bfloat16), 'tensor').astype(jnp.float32)  28.6 us
    concatenate x1, other arithmetic, local(): jnp.concatenate([forward, backward, outward], axis=1).astype(jnp.bfloat16)  25.2 us
    unnamed x21, local copies, waits for them, and re-layouts  16.8 us
    dot_general x1, matrix products, local(): forward = jnp.dot(acts, left_weights, preferred_element_type=jnp.float32)  14.2 us
    all_gather x1, blocking collectives, add_all(): parts = lax.all_gather(x, axis)  14 us
    dot_general x1, matrix products, local(): lax.dot_general(out_grad, w_down, contract_last, preferred_element_type=j...  9.66 us
    all_gather x1, blocking collectives, local(): query = lax.all_gather(own_query, 'example', axis=0, tiled=True)  8.55 us
  transfers between devices with their start and end apart: 1, of which 1 were waited for; matrix products, arithmetic and copies ran while one was open for 2% of the time, Pallas kernels for 0%

profile of v1, /device:TPU:0, one launch (start us, length us, event | category | flops | bytes accessed | tf_op | source)
XLA Modules:
  0.0 210.2 jit_solution(4972413996696922291)
XLA Ops:
  6.5 0.0 copy-start
  6.5 0.0 reduce-scatter.4.cloned.1.call-start
  6.5 2.1 %copy.17 = bf16[2048,64]{1,0:T(8,128)(2,1)} copy(bf16[2048,64]{0,1:T(8,128)(2,1)} %param.17) | data formatting | bytes 524288 | tf_op args[5]
  8.6 0.0 copy-start.2
  8.6 0.0 copy-start.4
  8.7 0.0 copy-start.3
  8.7 0.0 copy-start.5
  8.7 9.7 %convolution_convert_fusion = bf16[256,3584]{0,1:T(8,128)(2,1)S(1)} fusion(bf16[256,2048]{1,0:T(8,128)(2,1)} %param.13, bf16[3584,2048]{1,0:T(8,128)(2,1)} %param.16), kind=kOutput, calls=%fused_computation.10 | convolution fusion | flops 3759013888 | bytes 17563648 | tf_op jit(solution)/shard_map/dot_general | solution.py:64
  18.3 0.0 copy-done.2
  18.3 0.0 copy-done.4
  18.3 0.4 convolution_convert_fusion.1
  18.8 0.0 copy-done.3
  18.8 0.0 copy-done.5
  18.8 14.2 %fusion.9 = bf16[256,7232]{0,1:T(8,128)(2,1)S(1)} fusion(bf16[256,2048]{1,0:T(8,128)(2,1)S(1)} %copy-done.5, bf16[2048,64]{1,0:T(8,128)(2,1)S(1)} %copy-done.3, bf16[2048,3584]{1,0:T(8,128)(2,1)} %param.15, bf16[2048,3584]{1,0:T(8,128)(2,1)} %param.14), kind=kOutput, calls=%fused_computation.8 | convolution fusion | flops 7674019840 | bytes 34373632 | tf_op jit(solution)/shard_map/dot_general | solution.py:63
  33.0 25.2 %pad_maximum_fusion = bf16[256,10880]{0,1:T(8,128)(2,1)} fusion(bf16[256,64]{0,1:T(8,128)(2,1)S(1)} %convolution_convert_fusion.1, bf16[256,3584]{0,1:T(8,128)(2,1)S(1)} %convolution_convert_fusion, bf16[256,7232]{0,1:T(8,128)(2,1)S(1)} %fusion.9), kind=kLoop, calls=%fused_computation.9 | loop fusion | flops 16711680 | bytes 11141120 | tf_op jit(solution)/shard_map/concatenate | solution.py:67
  58.3 8.3 %copy.20 = bf16[256,10880]{1,0:T(8,128)(2,1)} copy(bf16[256,10880]{0,1:T(8,128)(2,1)} %pad_maximum_fusion) | data formatting | bytes 11141120
  66.6 0.0 copy-start.8
  66.6 0.0 reduce-scatter.4.cloned.1.call-update
  66.6 0.6 copy-done.8
  67.3 0.0 copy-done
  67.3 4.2 %gather_fusion = bf16[128,12288]{1,0:T(8,128)(2,1)} fusion(bf16[128,12288]{1,0:T(8,128)(2,1)S(1)} %copy-done, s32[1024]{0:T(1024)S(1)} %pad_clamp_fusion), kind=kCustom, calls=%fused_computation | custom fusion | bytes 6291968 | tf_op jit(solution)/shard_map/jit(_take)/gather | solution.py:88
  71.5 62.2 %reduce-scatter.4.cloned.1.call-done = bf16[64,10880]{1,0:T(8,128)(2,1)} async-done(((bf16[256,10880]{1,0:T(8,128)(2,1)}), bf16[64,10880]{1,0:T(8,128)(2,1)}) %reduce-scatter.4.cloned.1.call-update) | async-done | bytes 1392656
  133.6 4.0 %copy.21 = bf16[64,10880]{0,1:T(8,128)(2,1)} copy(bf16[64,10880]{1,0:T(8,128)(2,1)} %reduce-scatter.4.cloned.1.call-done) | data formatting | bytes 2785280
  137.6 0.0 copy-start.6
  137.6 2.0 convert_element_type.36
  139.6 0.0 copy-done.6
  139.6 0.0 copy-start.1
  139.7 0.0 copy-start.7
  139.7 0.7 convolution_convert_fusion.3
  140.4 1.7 copy-done.1
  142.1 0.0 copy-done.7
  142.1 0.9 convolution_convert_fusion.4
  143.0 28.6 %all-reduce = (bf16[64,64]{1,0:T(8,128)(2,1)S(1)}, bf16[64,64]{1,0:T(8,128)(2,1)S(1)}) all-reduce(bf16[64,64]{1,0:T(8,128)(2,1)S(1)} %convolution_convert_fusion.3, bf16[64,64]{1,0:T(8,128)(2,1)S(1)} %convolution_convert_fusion.4), channel_id=1, replica_groups=mesh['tensor'=8,'example'=4] {'tensor'}, use_global_device_ids=true, to_apply=%region_2.0 | all-reduce | flops 8192 | bytes 32768 | tf_op jit(solution)/shard_map/psum | solution.py:83
  171.6 0.8 convolution_convert_fusion.7
  172.4 0.1 concatenate.27
  172.5 0.8 convolution_convert_fusion.6
  173.4 0.1 concatenate.28
  173.5 2.8 %convolution_convert_fusion.2 = bf16[64,64]{1,0:T(8,128)(2,1)S(1)} fusion(bf16[3584,64]{0,1:T(8,128)(2,1)} %param.20, f32[64,10880]{0,1:T(8,128)} %copy-done.1), kind=kOutput, calls=%fused_computation.20 | convolution fusion | flops 30740480 | bytes 4136960 | tf_op jit(solution)/shard_map/dot_general | solution.py:80
  176.3 14.0 %all-gather = bf16[512,64]{1,0:T(8,128)(2,1)S(1)} all-gather(bf16[64,64]{1,0:T(8,128)(2,1)S(1)} %convolution_convert_fusion.2), channel_id=2, replica_groups=mesh['tensor'=8,'example'=4] {'tensor'}, dimensions={0}, use_global_device_ids=true | all-gather | bytes 73728 | tf_op jit(solution)/shard_map/all_gather | solution.py:10
  190.3 0.9 convolution_convert_fusion.5
  191.2 0.1 concatenate.29
  191.3 0.1 maximum_bitcast_fusion
  191.3 8.5 %all-gather.1 = bf16[4,1,12288]{2,1,0:T(2,128)(2,1)S(1)} all-gather(bf16[1,1,12288]{2,1,0:T(2,128)(2,1)S(1)} %maximum_bitcast_fusion), channel_id=1, replica_groups=mesh['tensor'=8,'example'=4] {'example'}, dimensions={0}, use_global_device_ids=true | all-gather | bytes 122880 | tf_op jit(solution)/shard_map/all_gather | solution.py:87
  199.9 3.5 %fusion.12 = f32[4,128]{1,0:T(4,128)} fusion(bf16[128,12288]{1,0:T(8,128)(2,1)} %gather_fusion, pred[128]{0:T(512)(128)(4,1)S(1)} %compare_and_fusion, bf16[4,1,12288]{2,1,0:T(2,128)(2,1)S(1)} %all-gather.1), kind=kOutput, calls=%fused_computation.11 | convolution fusion | flops 14155776 | bytes 3246208 | tf_op jit(solution)/shard_map/dot_general | solution.py:89
  (4 shorter events, 0.1 us)
Async XLA Ops:
  6.5 60.7 %copy-start = (bf16[128,12288]{1,0:T(8,128)(2,1)S(1)}, bf16[128,12288]{1,0:T(8,128)(2,1)}, u32[]{:S(2)}) copy-start(bf16[128,12288]{1,0:T(8,128)(2,1)} %param.22) | copy-start | bytes 9437188
  6.5 127.1 %reduce-scatter.4.cloned.1.call-start = ((), (), s32[]{:S(2)}) async-start(), calls=%async_computation.1 | async-start | bytes 6963200
  8.6 9.7 %copy-start.2 = (bf16[256,2048]{1,0:T(8,128)(2,1)S(1)}, bf16[256,2048]{1,0:T(8,128)(2,1)}, u32[]{:S(2)}) copy-start(bf16[256,2048]{1,0:T(8,128)(2,1)} %param.13) | copy-start | bytes 3145732
  8.6 9.7 %copy-start.4 = (bf16[2048,64]{0,1:T(8,128)(2,1)S(1)}, bf16[2048,64]{0,1:T(8,128)(2,1)}, u32[]{:S(2)}) copy-start(bf16[2048,64]{0,1:T(8,128)(2,1)} %param.21) | copy-start | bytes 786436
  8.7 10.1 %copy-start.3 = (bf16[2048,64]{1,0:T(8,128)(2,1)S(1)}, bf16[2048,64]{1,0:T(8,128)(2,1)}, u32[]{:S(2)}) copy-start(bf16[2048,64]{1,0:T(8,128)(2,1)} %copy.17) | copy-start | bytes 786436
  8.7 10.1 %copy-start.5 = (bf16[256,2048]{1,0:T(8,128)(2,1)S(1)}, bf16[256,2048]{1,0:T(8,128)(2,1)}, u32[]{:S(2)}) copy-start(bf16[256,2048]{1,0:T(8,128)(2,1)} %param.12) | copy-start | bytes 3145732
  66.6 0.7 copy-start.8
  137.6 2.0 copy-start.6
  139.6 2.5 %copy-start.1 = (f32[64,10880]{0,1:T(8,128)}, f32[64,10880]{0,1:T(8,128)S(1)}, u32[]{:S(2)}) copy-start(f32[64,10880]{0,1:T(8,128)S(1)} %convert_element_type.36) | copy-start | bytes 8355844
  139.7 2.4 %copy-start.7 = (bf16[3584,64]{0,1:T(8,128)(2,1)S(1)}, bf16[3584,64]{0,1:T(8,128)(2,1)}, u32[]{:S(2)}) copy-start(bf16[3584,64]{0,1:T(8,128)(2,1)} %param.18) | copy-start | bytes 1376260
Sparse Core Ops, SparseCore 0:
  66.7 66.8 reduce-scatter.3
